TPU v7x, 512 devices: a whole 4x8x8 slice. The times are simulated.
512 devices in a mesh: seq: 64 (over y, z_lo, core), tensor: 8 (over z_hi, x).
Axes of the slice: x: 4, y: 8, z: 8 (z_hi: 2, z_lo: 4; z = z_hi * 4 + z_lo), core: 2. Of those that a mesh axis runs over, the one named last changes fastest.
Arguments:
- queries: bfloat16 [16384, 3072], P('seq', 'tensor'), may hold values from -100 to 100
- key_tiles: bfloat16 [16384, 3072], P('seq', 'tensor'), may hold values from -6 to 6
- value_tiles: bfloat16 [16384, 3072], P('seq', 'tensor'), may hold values from -6 to 6
- cache_keys: bfloat16 [128, 128, 3072], P('seq', None, 'tensor'), may hold values from -6 to 6
- cache_values: bfloat16 [128, 128, 3072], P('seq', None, 'tensor'), may hold values from -6 to 6
- hidden: bfloat16 [16384, 5120], P('seq', 'tensor'), may hold values from -6 to 6
- out_weight: bfloat16 [3072, 5120], P('seq', 'tensor'), may hold values from -0.21875 to 0.21875
- gate_table: float32 [1000, 5120], P(None, 'tensor'), may hold values from 0.3 to 2.5
- lengths: int32 [16], replicated, may hold values from 512 to 1536, as said below
- page_table: int32 [16, 4], replicated, may hold values from 0 to 127, as said below
- page_count: int32 [16], replicated, may hold values from 0 to 4
- timestep: int32 [16], replicated, may hold values from 0 to 999
Outputs:
- layer_out: bfloat16 [16384, 5120], P('seq', 'tensor')
Inputs may be any that keep to these rules, and one draw needn't show every extreme that they name: The lengths sum to 16384. `page_table`: a page named by clip c lies on a seq index that holds some token of clip c (page p lies on seq index p // 2); a page may be named by several clips or twice.
All inputs are finite; a program needn't handle non-finite values.
Results may differ from a plain program's by a relative error of at most 0.018.
Values may be sent and summed in bfloat16 or wider, within the bound.
No kernel may reach another device: no remote copies, remote signals or barrier semaphores. Data moves between devices by JAX's collectives and lax.ppermute only.
A program may use at most 64 MiB of HBM per device.

v0:
```python
import math
import jax
import jax.numpy as jnp
from jax import lax
from jax.sharding import PartitionSpec as P

HD = 128
PAGE = 128
POOL = 2
REACH = 6
low_score = -1e30


def shifted(block, axis, distance):
    devices = range(lax.axis_size(axis))
    route = [(i - distance, i) for i in devices if i - distance in devices]
    return lax.ppermute(block, axis, route)


def clip_index(positions, clip_ends):
    return jnp.sum((positions[:, None] >= clip_ends[None, :]).astype(jnp.int32), axis=1)


def allowed_keys(query_clip, source, clip_ends, page_table, page_count, block_total, row_count):
    key_pos = source * row_count + jnp.arange(row_count, dtype=jnp.int32)
    in_range = (source >= 0) & (source < block_total)
    same_clip = (query_clip[:, None] == clip_index(key_pos, clip_ends)[None, :]) & in_range
    clip_total = clip_ends.shape[0]
    page_ids = source * POOL + jnp.arange(POOL, dtype=jnp.int32)
    live_slots = jnp.arange(page_table.shape[1], dtype=jnp.int32)[None, :] < page_count[:, None]
    named_pages = jnp.any(
        live_slots[:, :, None] & (page_table[:, :, None] == page_ids[None, None, :]), axis=1
    )
    member = query_clip[:, None] == jnp.arange(clip_total, dtype=jnp.int32)[None, :]
    page_ok = jnp.any(member[:, :, None] & named_pages[None], axis=1) & in_range
    page_ok = jnp.repeat(page_ok, PAGE, axis=1)
    return jnp.concatenate([same_clip, page_ok], axis=1)


def attend(carry_state, query_heads, key_heads, value_heads, allowed):
    running_max, totals, accumulated = carry_state
    scores = jnp.einsum(
        "qhd,khd->hqk", query_heads, key_heads, preferred_element_type=jnp.float32
    ) * (1.0 / math.sqrt(HD))
    scores = jnp.where(allowed[None], scores, low_score)
    new_max = jnp.maximum(running_max, jnp.max(scores, axis=2))
    factor = jnp.exp(running_max - new_max)
    weights = jnp.where(allowed[None], jnp.exp(scores - new_max[:, :, None]), 0.0)
    totals = totals * factor + jnp.sum(weights, axis=2)
    accumulated = accumulated * factor[:, :, None] + jnp.einsum(
        "hqk,khd->hqd",
        weights.astype(jnp.bfloat16),
        value_heads,
        preferred_element_type=jnp.float32,
    )
    return (new_max, totals, accumulated)


def empty_state(head_count, row_count):
    return (
        jnp.full((head_count, row_count), low_score, jnp.float32),
        jnp.zeros((head_count, row_count), jnp.float32),
        jnp.zeros((head_count, row_count, HD), jnp.float32),
    )


def visit_block(carry_state, packed, source, query_heads, query_clip, context):
    clip_ends, page_table, page_count, block_total = context
    row_count = query_heads.shape[0]
    head_count = query_heads.shape[1]
    allowed = allowed_keys(
        query_clip, source, clip_ends, page_table, page_count, block_total, row_count
    )
    key_heads = packed[0].reshape(-1, head_count, HD)
    value_heads = packed[1].reshape(-1, head_count, HD)
    return attend(carry_state, query_heads, key_heads, value_heads, allowed)


def fetch_direct(packed, offset):
    return shifted(packed, "seq", offset)


def local(
    queries,
    key_tiles,
    value_tiles,
    cache_keys,
    cache_values,
    hidden,
    out_weight,
    gate_table,
    lengths,
    page_table,
    page_count,
    timestep,
):
    row_count = queries.shape[0]
    tile_width = queries.shape[1]
    head_count = tile_width // HD
    block_total = lax.axis_size("seq")
    seq_index = lax.axis_index("seq")
    clip_ends = jnp.cumsum(lengths, dtype=jnp.int32)
    row_ids = jnp.arange(row_count, dtype=jnp.int32)
    positions = seq_index * row_count + row_ids
    query_clip = clip_index(positions, clip_ends)
    query_heads = queries.reshape(row_count, head_count, HD)
    context = (clip_ends, page_table, page_count, block_total)
    packed = jnp.stack(
        [
            jnp.concatenate([key_tiles, cache_keys.reshape(-1, tile_width)], axis=0),
            jnp.concatenate([value_tiles, cache_values.reshape(-1, tile_width)], axis=0),
        ]
    )
    carry_state = visit_block(
        empty_state(head_count, row_count), packed, seq_index, query_heads, query_clip, context
    )
    for offset in range(1, REACH + 1):
        from_below = fetch_direct(packed, offset)
        carry_state = visit_block(
            carry_state, from_below, seq_index - offset, query_heads, query_clip, context
        )
        from_above = fetch_direct(packed, -offset)
        carry_state = visit_block(
            carry_state, from_above, seq_index + offset, query_heads, query_clip, context
        )
    running_max, totals, accumulated = carry_state
    result = accumulated / totals[:, :, None]
    attention_local = (
        jnp.transpose(result, (1, 0, 2)).reshape(row_count, tile_width).astype(jnp.bfloat16)
    )
    attention = lax.all_gather(attention_local, "tensor", axis=1, tiled=True)
    projected = jnp.dot(
        attention,
        lax.all_gather(out_weight, "seq", axis=0, tiled=True),
        preferred_element_type=jnp.float32,
    )
    clip_total = lengths.shape[0]
    step_onehot = (
        timestep[:, None] == jnp.arange(gate_table.shape[0], dtype=jnp.int32)[None, :]
    ).astype(jnp.float32)
    clip_gate = jnp.dot(
        step_onehot, gate_table, precision=lax.Precision.HIGHEST, preferred_element_type=jnp.float32
    )
    clip_onehot = (query_clip[:, None] == jnp.arange(clip_total, dtype=jnp.int32)[None, :]).astype(
        jnp.float32
    )
    token_gate = jnp.dot(
        clip_onehot, clip_gate, precision=lax.Precision.HIGHEST, preferred_element_type=jnp.float32
    )
    return (hidden.astype(jnp.float32) + token_gate * projected).astype(jnp.bfloat16)


def solution(mesh):
    return jax.shard_map(
        local,
        mesh=mesh,
        in_specs=(
            P("seq", "tensor"),
            P("seq", "tensor"),
            P("seq", "tensor"),
            P("seq", None, "tensor"),
            P("seq", None, "tensor"),
            P("seq", "tensor"),
            P("seq", "tensor"),
            P(None, "tensor"),
            P(),
            P(),
            P(),
            P(),
        ),
        out_specs=P("seq", "tensor"),
        check_vma=False,
    )
```

profile of v0, /device:TPU:1, one launch (start us, length us, event | category | flops | bytes accessed | tf_op | source)
XLA Modules:
  0.0 506.3 jit_solution(10120251715169249315)
XLA Ops:
  6.5 1.2 copy.107
  7.8 1.1 copy.113
  8.8 1.1 copy.196
  10.0 1.1 copy.197
  11.1 1.0 pad_maximum_fusion
  12.1 1.3 collective-permute-start.9
  13.4 10.5 %collective-permute-start.8 = (bf16[2,512,384]{1,2,0:T(8,128)(2,1)}, bf16[2,512,384]{1,2,0:T(8,128)(2,1)}, u32[]{:S(2)}, u32[]{:S(2)}) collective-permute-start(bf16[2,512,384]{1,2,0:T(8,128)(2,1)} %pad_maximum_fusion), channel_id=1, source_target_pairs={{0,40},{8,48},{16,56},{24,64},{32,72},{40,80},{48,88},{56,96},{64,... | collective-permute-start | bytes 2359304 | tf_op jit(solution)/shard_map/ppermute | solution.py:17
  23.9 1.3 collective-permute-start.7
  25.2 5.8 %collective-permute-start.6 = (bf16[2,512,384]{1,2,0:T(8,128)(2,1)}, bf16[2,512,384]{1,2,0:T(8,128)(2,1)}, u32[]{:S(2)}, u32[]{:S(2)}) collective-permute-start(bf16[2,512,384]{1,2,0:T(8,128)(2,1)} %pad_maximum_fusion), channel_id=1, source_target_pairs={{0,32},{8,40},{16,48},{24,56},{32,64},{40,72},{48,80},{56,88},{64,... | collective-permute-start | bytes 2359304 | tf_op jit(solution)/shard_map/ppermute | solution.py:17
  31.0 1.3 collective-permute-start.5
  32.8 0.7 convert_reduce_fusion
  33.5 1.1 copy.111
  34.6 0.8 copy.109
  35.4 0.7 copy.110
  36.3 0.7 and_reduce_fusion
  38.1 0.7 pad_add_fusion.4
  38.8 0.7 pad_add_fusion.3
  39.5 0.7 pad_add_fusion.2
  40.1 0.7 broadcast_and_fusion.12
  40.8 0.9 compare_and_fusion.1
  41.8 2.6 fusion.175
  44.5 0.7 pad_add_fusion.11
  45.2 0.7 pad_add_fusion.1
  45.9 0.7 pad_add_fusion.12
  46.5 1.8 copy.114
  48.3 1.7 concatenate.64
  50.0 5.2 %collective-permute-start.4 = (bf16[2,512,384]{1,2,0:T(8,128)(2,1)}, bf16[2,512,384]{1,2,0:T(8,128)(2,1)S(1)}, u32[]{:S(2)}, u32[]{:S(2)}) collective-permute-start(bf16[2,512,384]{1,2,0:T(8,128)(2,1)} %pad_maximum_fusion), channel_id=1, source_target_pairs={{0,24},{8,32},{16,40},{24,48},{32,56},{40,64},{48,72},{56,80},{64,... | collective-permute-start | bytes 2359304 | tf_op jit(solution)/shard_map/ppermute | solution.py:17
  55.2 1.2 fusion.153
  56.4 64.8 %collective-permute-done.8 = bf16[2,512,384]{1,2,0:T(8,128)(2,1)} collective-permute-done((bf16[2,512,384]{1,2,0:T(8,128)(2,1)}, bf16[2,512,384]{1,2,0:T(8,128)(2,1)}, u32[]{:S(2)}, u32[]{:S(2)}) %collective-permute-start.8) | collective-permute-done | bytes 786464 | tf_op jit(solution)/shard_map/ppermute | solution.py:17
  121.2 1.3 collective-permute-start.3
  122.5 1.2 fusion.154
  123.7 4.0 collective-permute-start.2
  127.7 1.2 fusion.155
  128.9 9.2 %collective-permute-done.6 = bf16[2,512,384]{1,2,0:T(8,128)(2,1)} collective-permute-done((bf16[2,512,384]{1,2,0:T(8,128)(2,1)}, bf16[2,512,384]{1,2,0:T(8,128)(2,1)}, u32[]{:S(2)}, u32[]{:S(2)}) %collective-permute-start.6) | collective-permute-done | bytes 786464 | tf_op jit(solution)/shard_map/ppermute | solution.py:17
  138.0 43.7 %collective-permute-start.1 = (bf16[2,512,384]{1,2,0:T(8,128)(2,1)}, bf16[2,512,384]{1,2,0:T(8,128)(2,1)S(1)}, u32[]{:S(2)}, u32[]{:S(2)}) collective-permute-start(bf16[2,512,384]{1,2,0:T(8,128)(2,1)} %pad_maximum_fusion), channel_id=1, source_target_pairs={{8,0},{16,8},{24,16},{32,24},{40,32},{48,40},{56,48},{64,56},{72,6... | collective-permute-start | bytes 2359304 | tf_op jit(solution)/shard_map/ppermute | solution.py:17
  181.7 1.2 fusion.156
  182.9 23.6 %collective-permute-start.10 = (bf16[2,512,384]{1,2,0:T(8,128)(2,1)}, bf16[2,512,384]{1,2,0:T(8,128)(2,1)S(1)}, u32[]{:S(2)}, u32[]{:S(2)}) collective-permute-start(bf16[2,512,384]{1,2,0:T(8,128)(2,1)} %pad_maximum_fusion), channel_id=1, source_target_pairs={{0,48},{8,56},{16,64},{24,72},{32,80},{40,88},{48,96},{56,104},{64... | collective-permute-start | bytes 2359304 | tf_op jit(solution)/shard_map/ppermute | solution.py:17
  206.5 1.2 fusion.157
  207.7 34.8 %collective-permute-start = (bf16[2,512,384]{1,2,0:T(8,128)(2,1)}, bf16[2,512,384]{1,2,0:T(8,128)(2,1)S(1)}, u32[]{:S(2)}, u32[]{:S(2)}) collective-permute-start(bf16[2,512,384]{1,2,0:T(8,128)(2,1)} %pad_maximum_fusion), channel_id=1, source_target_pairs={{0,8},{8,16},{16,24},{24,32},{32,40},{40,48},{48,56},{56,64},{64,7... | collective-permute-start | bytes 2359304 | tf_op jit(solution)/shard_map/ppermute | solution.py:17
  243.1 1.5 collective-permute-start.11
  249.5 19.1 %collective-permute-done = bf16[2,512,384]{1,2,0:T(8,128)(2,1)S(1)} collective-permute-done((bf16[2,512,384]{1,2,0:T(8,128)(2,1)}, bf16[2,512,384]{1,2,0:T(8,128)(2,1)S(1)}, u32[]{:S(2)}, u32[]{:S(2)}) %collective-permute-start) | collective-permute-done | bytes 786464 | tf_op jit(solution)/shard_map/ppermute | solution.py:17
  278.4 0.7 fusion.47
  281.4 1.1 fusion.54
  282.6 0.7 all-gather.5.cloned.1.call-update
  283.3 0.9 fusion.113
  284.8 89.4 %all-gather.3.cloned.1.call-done = bf16[256,3072]{0,1:T(8,128)(2,1)} async-done(((bf16[256,384]{0,1:T(8,128)(2,1)}), bf16[256,3072]{0,1:T(8,128)(2,1)}) %all-gather.3.cloned.1.call-update) | async-done | bytes 1572880 | tf_op jit(solution)/shard_map/all_gather | solution.py:131
  374.2 120.5 %all-gather.5.cloned.1.call-done = bf16[3072,640]{1,0:T(8,128)(2,1)} async-done(((bf16[48,640]{1,0:T(8,128)(2,1)}), bf16[3072,640]{1,0:T(8,128)(2,1)}) %all-gather.5.cloned.1.call-update) | async-done | bytes 3932176 | tf_op jit(solution)/shard_map/all_gather | solution.py:134
  494.7 4.7 fusion.27
  (156 shorter events, 19.5 us)
Async XLA Ops:
  6.5 276.8 %copy-start = (f32[1000,640]{1,0:T(8,128)S(1)}, f32[1000,640]{1,0:T(8,128)}, u32[]{:S(2)}) copy-start(f32[1000,640]{1,0:T(8,128)} %param.19) | copy-start | bytes 7680004
  6.5 367.7 %all-gather.3.cloned.1.call-start = ((), (), s32[]{:S(2)}) async-start(), calls=%async_computation | async-start | bytes 1769472 | tf_op jit(solution)/shard_map/all_gather | solution.py:131
  8.8 3.3 copy-start.9
  11.0 21.4 %copy-start.8 = (bf16[2,128,384]{2,1,0:T(8,128)(2,1)S(1)}, bf16[2,128,384]{2,1,0:T(8,128)(2,1)}, u32[]{:S(2)}) copy-start(bf16[2,128,384]{2,1,0:T(8,128)(2,1)} %param.15) | copy-start | bytes 589828
  11.0 21.4 %copy-start.17 = (s32[16]{0:T(128)S(1)}, s32[16]{0:T(128)}, u32[]{:S(2)}) copy-start(s32[16]{0:T(128)} %param.20) | copy-start | bytes 196
  11.1 22.5 %copy-start.20 = (s32[16]{0:T(128)S(1)}, s32[16]{0:T(128)}, u32[]{:S(2)}) copy-start(s32[16]{0:T(128)} %param.22) | copy-start | bytes 196
  11.1 25.1 %copy-start.16 = (s32[16,4]{0,1:T(4,128)S(1)}, s32[16,4]{0,1:T(4,128)}, u32[]{:S(2)}) copy-start(s32[16,4]{0,1:T(4,128)} %param.21) | copy-start | bytes 772
  12.1 37.9 %collective-permute-start.9 = (bf16[2,512,384]{1,2,0:T(8,128)(2,1)}, bf16[2,512,384]{1,2,0:T(8,128)(2,1)}, u32[]{:S(2)}, u32[]{:S(2)}) collective-permute-start(bf16[2,512,384]{1,2,0:T(8,128)(2,1)} %pad_maximum_fusion), channel_id=1, source_target_pairs={{40,0},{48,8},{56,16},{64,24},{72,32},{80,40},{88,48},{96,56},{104... | collective-permute-start | bytes 2359304 | tf_op jit(solution)/shard_map/ppermute | solution.py:17
  13.4 107.8 %collective-permute-start.8 = (bf16[2,512,384]{1,2,0:T(8,128)(2,1)}, bf16[2,512,384]{1,2,0:T(8,128)(2,1)}, u32[]{:S(2)}, u32[]{:S(2)}) collective-permute-start(bf16[2,512,384]{1,2,0:T(8,128)(2,1)} %pad_maximum_fusion), channel_id=1, source_target_pairs={{0,40},{8,48},{16,56},{24,64},{32,72},{40,80},{48,88},{56,96},{64,... | collective-permute-start | bytes 2359304 | tf_op jit(solution)/shard_map/ppermute | solution.py:17
  23.9 99.7 %collective-permute-start.7 = (bf16[2,512,384]{1,2,0:T(8,128)(2,1)}, bf16[2,512,384]{1,2,0:T(8,128)(2,1)}, u32[]{:S(2)}, u32[]{:S(2)}) collective-permute-start(bf16[2,512,384]{1,2,0:T(8,128)(2,1)} %pad_maximum_fusion), channel_id=1, source_target_pairs={{32,0},{40,8},{48,16},{56,24},{64,32},{72,40},{80,48},{88,56},{96,... | collective-permute-start | bytes 2359304 | tf_op jit(solution)/shard_map/ppermute | solution.py:17
  25.2 112.8 %collective-permute-start.6 = (bf16[2,512,384]{1,2,0:T(8,128)(2,1)}, bf16[2,512,384]{1,2,0:T(8,128)(2,1)}, u32[]{:S(2)}, u32[]{:S(2)}) collective-permute-start(bf16[2,512,384]{1,2,0:T(8,128)(2,1)} %pad_maximum_fusion), channel_id=1, source_target_pairs={{0,32},{8,40},{16,48},{24,56},{32,64},{40,72},{48,80},{56,88},{64,... | collective-permute-start | bytes 2359304 | tf_op jit(solution)/shard_map/ppermute | solution.py:17
  31.0 151.9 %collective-permute-start.5 = (bf16[2,512,384]{1,2,0:T(8,128)(2,1)}, bf16[2,512,384]{1,2,0:T(8,128)(2,1)}, u32[]{:S(2)}, u32[]{:S(2)}) collective-permute-start(bf16[2,512,384]{1,2,0:T(8,128)(2,1)} %pad_maximum_fusion), channel_id=1, source_target_pairs={{24,0},{32,8},{40,16},{48,24},{56,32},{64,40},{72,48},{80,56},{88,... | collective-permute-start | bytes 2359304 | tf_op jit(solution)/shard_map/ppermute | solution.py:17
  40.8 3.6 copy-start.15
  40.8 3.6 copy-start.14
  41.8 4.0 copy-start.11
  50.0 157.7 %collective-permute-start.4 = (bf16[2,512,384]{1,2,0:T(8,128)(2,1)}, bf16[2,512,384]{1,2,0:T(8,128)(2,1)S(1)}, u32[]{:S(2)}, u32[]{:S(2)}) collective-permute-start(bf16[2,512,384]{1,2,0:T(8,128)(2,1)} %pad_maximum_fusion), channel_id=1, source_target_pairs={{0,24},{8,32},{16,40},{24,48},{32,56},{40,64},{48,72},{56,80},{64,... | collective-permute-start | bytes 2359304 | tf_op jit(solution)/shard_map/ppermute | solution.py:17
  121.2 121.9 %collective-permute-start.3 = (bf16[2,512,384]{1,2,0:T(8,128)(2,1)}, bf16[2,512,384]{1,2,0:T(8,128)(2,1)S(1)}, u32[]{:S(2)}, u32[]{:S(2)}) collective-permute-start(bf16[2,512,384]{1,2,0:T(8,128)(2,1)} %pad_maximum_fusion), channel_id=1, source_target_pairs={{16,0},{24,8},{32,16},{40,24},{48,32},{56,40},{64,48},{72,56},{80,... | collective-permute-start | bytes 2359304 | tf_op jit(solution)/shard_map/ppermute | solution.py:17
  123.7 121.9 %collective-permute-start.2 = (bf16[2,512,384]{1,2,0:T(8,128)(2,1)}, bf16[2,512,384]{1,2,0:T(8,128)(2,1)S(1)}, u32[]{:S(2)}, u32[]{:S(2)}) collective-permute-start(bf16[2,512,384]{1,2,0:T(8,128)(2,1)} %pad_maximum_fusion), channel_id=1, source_target_pairs={{0,16},{8,24},{16,32},{24,40},{32,48},{40,56},{48,64},{56,72},{64,... | collective-permute-start | bytes 2359304 | tf_op jit(solution)/shard_map/ppermute | solution.py:17
  138.0 108.6 %collective-permute-start.1 = (bf16[2,512,384]{1,2,0:T(8,128)(2,1)}, bf16[2,512,384]{1,2,0:T(8,128)(2,1)S(1)}, u32[]{:S(2)}, u32[]{:S(2)}) collective-permute-start(bf16[2,512,384]{1,2,0:T(8,128)(2,1)} %pad_maximum_fusion), channel_id=1, source_target_pairs={{8,0},{16,8},{24,16},{32,24},{40,32},{48,40},{56,48},{64,56},{72,6... | collective-permute-start | bytes 2359304 | tf_op jit(solution)/shard_map/ppermute | solution.py:17
  182.9 65.2 %collective-permute-start.10 = (bf16[2,512,384]{1,2,0:T(8,128)(2,1)}, bf16[2,512,384]{1,2,0:T(8,128)(2,1)S(1)}, u32[]{:S(2)}, u32[]{:S(2)}) collective-permute-start(bf16[2,512,384]{1,2,0:T(8,128)(2,1)} %pad_maximum_fusion), channel_id=1, source_target_pairs={{0,48},{8,56},{16,64},{24,72},{32,80},{40,88},{48,96},{56,104},{64... | collective-permute-start | bytes 2359304 | tf_op jit(solution)/shard_map/ppermute | solution.py:17
  207.7 60.9 %collective-permute-start = (bf16[2,512,384]{1,2,0:T(8,128)(2,1)}, bf16[2,512,384]{1,2,0:T(8,128)(2,1)S(1)}, u32[]{:S(2)}, u32[]{:S(2)}) collective-permute-start(bf16[2,512,384]{1,2,0:T(8,128)(2,1)} %pad_maximum_fusion), channel_id=1, source_target_pairs={{0,8},{8,16},{16,24},{24,32},{32,40},{40,48},{48,56},{56,64},{64,7... | collective-permute-start | bytes 2359304 | tf_op jit(solution)/shard_map/ppermute | solution.py:17
  243.1 26.6 %collective-permute-start.11 = (bf16[2,512,384]{1,2,0:T(8,128)(2,1)}, bf16[2,512,384]{1,2,0:T(8,128)(2,1)S(1)}, u32[]{:S(2)}, u32[]{:S(2)}) collective-permute-start(bf16[2,512,384]{1,2,0:T(8,128)(2,1)} %pad_maximum_fusion), channel_id=1, source_target_pairs={{48,0},{56,8},{64,16},{72,24},{80,32},{88,40},{96,48},{104,56},{11... | collective-permute-start | bytes 2359304 | tf_op jit(solution)/shard_map/ppermute | solution.py:17
  246.6 0.9 copy-start.1
  247.6 0.9 copy-start.3
  248.0 0.9 copy-start.4
  249.0 19.7 %copy-start.2 = (pred[256,512]{0,1:T(8,128)(4,1)S(1)}, pred[256,512]{0,1:T(8,128)(4,1)}, u32[]{:S(2)}) copy-start(pred[256,512]{0,1:T(8,128)(4,1)} %pad_add_fusion.11) | copy-start | bytes 393220
  249.5 19.7 %copy-start.5 = (pred[256,512]{0,1:T(8,128)(4,1)S(1)}, pred[256,512]{0,1:T(8,128)(4,1)}, u32[]{:S(2)}) copy-start(pred[256,512]{0,1:T(8,128)(4,1)} %pad_add_fusion.1) | copy-start | bytes 393220
  269.2 0.9 copy-start.7
  269.7 1.4 copy-start.6
  269.7 1.4 copy-start.12
  274.6 0.9 copy-start.10
  274.6 1.0 copy-start.13
  281.4 1.9 copy-start.18
  282.6 212.2 %all-gather.5.cloned.1.call-start = ((), (), s32[]{:S(2)}) async-start(), calls=%async_computation.1 | async-start | bytes 3993600 | tf_op jit(solution)/shard_map/all_gather | solution.py:134
  283.3 211.4 %copy-start.19 = (bf16[256,640]{1,0:T(8,128)(2,1)S(1)}, bf16[256,640]{1,0:T(8,128)(2,1)}, u32[]{:S(2)}) copy-start(bf16[256,640]{1,0:T(8,128)(2,1)} %param.17) | copy-start | bytes 983044
Sparse Core Ops, SparseCore 0:
  282.7 91.4 all-gather.2
  376.3 118.3 all-gather.4
where the time goes:
time: 507 us; the launch traced here: 506 us
  waiting for transfers between devices  304 us (60%)
  starting transfers between devices  134 us (26%)
  matrix products  21.3 us (4%)
  local copies, waits for them, and re-layouts  19.2 us (4%)
  between operations  14.4 us (3%)
  other arithmetic  13.3 us (3%)
    ppermute x12, starting transfers between devices, shifted(): return lax.ppermute(block, axis, route)  134 us
    all_gather x1, waiting for transfers between devices, local(): lax.all_gather(out_weight, 'seq', axis=0, tiled=True)  121 us
    ppermute x12, waiting for transfers between devices, shifted(): return lax.ppermute(block, axis, route)  93.1 us
    all_gather x1, waiting for transfers between devices, local(): attention = lax.all_gather(attention_local, 'tensor', axis=1, tiled=True)  89.4 us
  transfers between devices with their start and end apart: 14, of which 5 were waited for; matrix products, arithmetic and copies ran while one was open for 6% of the time, Pallas kernels for 0%

commit v1 on v0

--- a/solution.py
+++ b/solution.py
@@ -131,7 +131,9 @@
     attention = lax.all_gather(attention_local, "tensor", axis=1, tiled=True)
     projected = jnp.dot(
         attention,
-        lax.all_gather(out_weight, "seq", axis=0, tiled=True),
+        jnp.concatenate(
+            lax.all_to_all(jnp.stack([out_weight] * lax.axis_size("seq")), "seq", 0, 0), axis=0
+        ),
         preferred_element_type=jnp.float32,
     )
     clip_total = lengths.shape[0]

time: 507 us -> 472 us (0.931)
  waiting for transfers between devices: 304 us -> 241 us
  starting transfers between devices: 134 us -> 159 us
    all_gather x1 -> x0, waiting for transfers between devices: 121 us -> none  [local(): lax.all_gather(out_weight, 'seq', axis=0, tiled=True)]
    ppermute x12, waiting for transfers between devices: 93.1 us -> 150 us  [shifted(): return lax.ppermute(block, axis, route)]
    all_to_all x0 -> x1, starting transfers between devices: none -> 14.2 us  [local(): lax.all_to_all(jnp.stack([out_weight] * lax.axis_size('seq')), 'seq', 0, 0)]
    ppermute x12, starting transfers between devices: 134 us -> 145 us  [shifted(): return lax.ppermute(block, axis, route)]
  transfers between devices with their start and end apart: 14 -> 14, of which waited for: 5 -> 4; matrix products, arithmetic and copies ran while one was open for 6% -> 9% of each run, Pallas kernels for 0% -> 0%
where the time goes in v1:
time: 472 us; the launch traced here: 471 us
  waiting for transfers between devices  241 us (51%)
  starting transfers between devices  159 us (34%)
  matrix products  21.4 us (5%)
  local copies, waits for them, and re-layouts  21.3 us (5%)
  between operations  14.4 us (3%)
  other arithmetic  13.3 us (3%)
    ppermute x12, waiting for transfers between devices, shifted(): return lax.ppermute(block, axis, route)  150 us
    ppermute x12, starting transfers between devices, shifted(): return lax.ppermute(block, axis, route)  145 us
    all_gather x1, waiting for transfers between devices, local(): attention = lax.all_gather(attention_local, 'tensor', axis=1, tiled=True)  90.7 us
    all_to_all x1, starting transfers between devices, local(): lax.all_to_all(jnp.stack([out_weight] * lax.axis_size('seq')), 'seq', 0, 0)  14.2 us
  transfers between devices with their start and end apart: 14, of which 4 were waited for; matrix products, arithmetic and copies ran while one was open for 9% of the time, Pallas kernels for 0%

profile of v1, /device:TPU:1, one launch (start us, length us, event | category | flops | bytes accessed | tf_op | source)
XLA Modules:
  0.0 470.7 jit_solution(18345485536869258591)
XLA Ops:
  6.5 1.2 copy.107
  7.8 1.1 copy.113
  8.8 1.1 copy.196
  10.0 1.1 copy.197
  11.1 1.0 pad_maximum_fusion
  12.1 1.3 collective-permute-start.9
  13.4 10.5 %collective-permute-start.8 = (bf16[2,512,384]{1,2,0:T(8,128)(2,1)}, bf16[2,512,384]{1,2,0:T(8,128)(2,1)}, u32[]{:S(2)}, u32[]{:S(2)}) collective-permute-start(bf16[2,512,384]{1,2,0:T(8,128)(2,1)} %pad_maximum_fusion), channel_id=1, source_target_pairs={{0,40},{8,48},{16,56},{24,64},{32,72},{40,80},{48,88},{56,96},{64,... | collective-permute-start | bytes 2359304 | tf_op jit(solution)/shard_map/ppermute | solution.py:17
  23.9 1.3 collective-permute-start.7
  25.2 5.8 %collective-permute-start.6 = (bf16[2,512,384]{1,2,0:T(8,128)(2,1)}, bf16[2,512,384]{1,2,0:T(8,128)(2,1)}, u32[]{:S(2)}, u32[]{:S(2)}) collective-permute-start(bf16[2,512,384]{1,2,0:T(8,128)(2,1)} %pad_maximum_fusion), channel_id=1, source_target_pairs={{0,32},{8,40},{16,48},{24,56},{32,64},{40,72},{48,80},{56,88},{64,... | collective-permute-start | bytes 2359304 | tf_op jit(solution)/shard_map/ppermute | solution.py:17
  31.0 1.3 collective-permute-start.5
  32.3 2.2 stack.11
  34.5 14.2 %all-to-all-start = ((bf16[64,48,640]{2,1,0:T(8,128)(2,1)}), bf16[64,48,640]{2,1,0:T(8,128)(2,1)}, u32[]{:S(2)}, u32[]{:S(2)}) async-start(bf16[64,48,640]{2,1,0:T(8,128)(2,1)} %stack.11), calls=%async_computation | async-start | bytes 7864320 | tf_op jit(solution)/shard_map/all_to_all | solution.py:135
  49.3 0.7 convert_reduce_fusion
  50.0 1.1 copy.111
  51.1 0.8 copy.109
  51.9 0.7 copy.110
  52.8 0.7 and_reduce_fusion
  54.6 0.6 pad_add_fusion.4
  55.2 0.7 pad_add_fusion.3
  55.9 0.7 pad_add_fusion.2
  56.6 0.6 broadcast_and_fusion.12
  57.2 0.9 compare_and_fusion.1
  58.2 2.7 fusion.175
  61.0 0.7 pad_add_fusion.11
  61.7 0.7 pad_add_fusion.1
  62.4 0.7 pad_add_fusion.12
  63.0 1.8 copy.114
  64.8 1.7 concatenate.64
  66.5 4.5 collective-permute-start.4
  71.0 1.2 fusion.153
  72.2 113.7 %collective-permute-done.8 = bf16[2,512,384]{1,2,0:T(8,128)(2,1)} collective-permute-done((bf16[2,512,384]{1,2,0:T(8,128)(2,1)}, bf16[2,512,384]{1,2,0:T(8,128)(2,1)}, u32[]{:S(2)}, u32[]{:S(2)}) %collective-permute-start.8) | collective-permute-done | bytes 786464 | tf_op jit(solution)/shard_map/ppermute | solution.py:17
  185.9 1.3 collective-permute-start.3
  187.2 1.2 fusion.154
  188.4 4.0 collective-permute-start.2
  192.5 1.2 fusion.155
  193.6 17.3 %collective-permute-done.6 = bf16[2,512,384]{1,2,0:T(8,128)(2,1)} collective-permute-done((bf16[2,512,384]{1,2,0:T(8,128)(2,1)}, bf16[2,512,384]{1,2,0:T(8,128)(2,1)}, u32[]{:S(2)}, u32[]{:S(2)}) %collective-permute-start.6) | collective-permute-done | bytes 786464 | tf_op jit(solution)/shard_map/ppermute | solution.py:17
  210.9 50.0 %collective-permute-start.1 = (bf16[2,512,384]{1,2,0:T(8,128)(2,1)}, bf16[2,512,384]{1,2,0:T(8,128)(2,1)S(1)}, u32[]{:S(2)}, u32[]{:S(2)}) collective-permute-start(bf16[2,512,384]{1,2,0:T(8,128)(2,1)} %pad_maximum_fusion), channel_id=1, source_target_pairs={{8,0},{16,8},{24,16},{32,24},{40,32},{48,40},{56,48},{64,56},{72,6... | collective-permute-start | bytes 2359304 | tf_op jit(solution)/shard_map/ppermute | solution.py:17
  260.9 1.2 fusion.156
  262.1 23.6 %collective-permute-start.10 = (bf16[2,512,384]{1,2,0:T(8,128)(2,1)}, bf16[2,512,384]{1,2,0:T(8,128)(2,1)S(1)}, u32[]{:S(2)}, u32[]{:S(2)}) collective-permute-start(bf16[2,512,384]{1,2,0:T(8,128)(2,1)} %pad_maximum_fusion), channel_id=1, source_target_pairs={{0,48},{8,56},{16,64},{24,72},{32,80},{40,88},{48,96},{56,104},{64... | collective-permute-start | bytes 2359304 | tf_op jit(solution)/shard_map/ppermute | solution.py:17
  285.7 1.2 fusion.157
  286.9 40.1 %collective-permute-start = (bf16[2,512,384]{1,2,0:T(8,128)(2,1)}, bf16[2,512,384]{1,2,0:T(8,128)(2,1)S(1)}, u32[]{:S(2)}, u32[]{:S(2)}) collective-permute-start(bf16[2,512,384]{1,2,0:T(8,128)(2,1)} %pad_maximum_fusion), channel_id=1, source_target_pairs={{0,8},{8,16},{16,24},{24,32},{32,40},{40,48},{48,56},{56,64},{64,7... | collective-permute-start | bytes 2359304 | tf_op jit(solution)/shard_map/ppermute | solution.py:17
  327.6 1.5 collective-permute-start.11
  333.9 19.1 %collective-permute-done = bf16[2,512,384]{1,2,0:T(8,128)(2,1)S(1)} collective-permute-done((bf16[2,512,384]{1,2,0:T(8,128)(2,1)}, bf16[2,512,384]{1,2,0:T(8,128)(2,1)S(1)}, u32[]{:S(2)}, u32[]{:S(2)}) %collective-permute-start) | collective-permute-done | bytes 786464 | tf_op jit(solution)/shard_map/ppermute | solution.py:17
  362.8 0.7 fusion.47
  365.8 1.1 fusion.54
  367.0 0.9 fusion.113
  368.4 90.7 %all-gather.2.cloned.1.call-done = bf16[256,3072]{0,1:T(8,128)(2,1)} async-done(((bf16[256,384]{0,1:T(8,128)(2,1)}), bf16[256,3072]{0,1:T(8,128)(2,1)}) %all-gather.2.cloned.1.call-update) | async-done | bytes 1572880 | tf_op jit(solution)/shard_map/all_gather | solution.py:131
  459.1 4.7 %fusion.27 = bf16[256,640]{1,0:T(8,128)(2,1)} fusion(f32[256,640]{1,0:T(8,128)S(1)} %fusion.146, bf16[256,3072]{0,1:T(8,128)(2,1)} %all-gather.2.cloned.1.call-done, bf16[3072,640]{1,0:T(8,128)(2,1)} %bitcast.98, bf16[256,640]{1,0:T(8,128)(2,1)S(1)} %copy-done.20), kind=kOutput, calls=%fused_computation.54 | convolution fusion | flops 1007288320 | bytes 6815744 | tf_op jit(solution)/shard_map/dot_general | solution.py:132
  (158 shorter events, 19.4 us)
Async XLA Ops:
  6.5 360.4 %copy-start = (f32[1000,640]{1,0:T(8,128)S(1)}, f32[1000,640]{1,0:T(8,128)}, u32[]{:S(2)}) copy-start(f32[1000,640]{1,0:T(8,128)} %param.19) | copy-start | bytes 7680004
  8.8 3.2 copy-start.9
  11.0 21.3 %copy-start.14 = (bf16[48,640]{1,0:T(8,128)(2,1)S(1)}, bf16[48,640]{1,0:T(8,128)(2,1)}, u32[]{:S(2)}) copy-start(bf16[48,640]{1,0:T(8,128)(2,1)} %param.18) | copy-start | bytes 184324
  12.1 54.5 %collective-permute-start.9 = (bf16[2,512,384]{1,2,0:T(8,128)(2,1)}, bf16[2,512,384]{1,2,0:T(8,128)(2,1)}, u32[]{:S(2)}, u32[]{:S(2)}) collective-permute-start(bf16[2,512,384]{1,2,0:T(8,128)(2,1)} %pad_maximum_fusion), channel_id=1, source_target_pairs={{40,0},{48,8},{56,16},{64,24},{72,32},{80,40},{88,48},{96,56},{104... | collective-permute-start | bytes 2359304 | tf_op jit(solution)/shard_map/ppermute | solution.py:17
  13.4 172.6 %collective-permute-start.8 = (bf16[2,512,384]{1,2,0:T(8,128)(2,1)}, bf16[2,512,384]{1,2,0:T(8,128)(2,1)}, u32[]{:S(2)}, u32[]{:S(2)}) collective-permute-start(bf16[2,512,384]{1,2,0:T(8,128)(2,1)} %pad_maximum_fusion), channel_id=1, source_target_pairs={{0,40},{8,48},{16,56},{24,64},{32,72},{40,80},{48,88},{56,96},{64,... | collective-permute-start | bytes 2359304 | tf_op jit(solution)/shard_map/ppermute | solution.py:17
  23.9 164.5 %collective-permute-start.7 = (bf16[2,512,384]{1,2,0:T(8,128)(2,1)}, bf16[2,512,384]{1,2,0:T(8,128)(2,1)}, u32[]{:S(2)}, u32[]{:S(2)}) collective-permute-start(bf16[2,512,384]{1,2,0:T(8,128)(2,1)} %pad_maximum_fusion), channel_id=1, source_target_pairs={{32,0},{40,8},{48,16},{56,24},{64,32},{72,40},{80,48},{88,56},{96,... | collective-permute-start | bytes 2359304 | tf_op jit(solution)/shard_map/ppermute | solution.py:17
  25.2 185.7 %collective-permute-start.6 = (bf16[2,512,384]{1,2,0:T(8,128)(2,1)}, bf16[2,512,384]{1,2,0:T(8,128)(2,1)}, u32[]{:S(2)}, u32[]{:S(2)}) collective-permute-start(bf16[2,512,384]{1,2,0:T(8,128)(2,1)} %pad_maximum_fusion), channel_id=1, source_target_pairs={{0,32},{8,40},{16,48},{24,56},{32,64},{40,72},{48,80},{56,88},{64,... | collective-permute-start | bytes 2359304 | tf_op jit(solution)/shard_map/ppermute | solution.py:17
  31.0 231.1 %collective-permute-start.5 = (bf16[2,512,384]{1,2,0:T(8,128)(2,1)}, bf16[2,512,384]{1,2,0:T(8,128)(2,1)}, u32[]{:S(2)}, u32[]{:S(2)}) collective-permute-start(bf16[2,512,384]{1,2,0:T(8,128)(2,1)} %pad_maximum_fusion), channel_id=1, source_target_pairs={{24,0},{32,8},{40,16},{48,24},{56,32},{64,40},{72,48},{80,56},{88,... | collective-permute-start | bytes 2359304 | tf_op jit(solution)/shard_map/ppermute | solution.py:17
  34.5 14.4 %copy-start.8 = (bf16[2,128,384]{2,1,0:T(8,128)(2,1)S(1)}, bf16[2,128,384]{2,1,0:T(8,128)(2,1)}, u32[]{:S(2)}) copy-start(bf16[2,128,384]{2,1,0:T(8,128)(2,1)} %param.15) | copy-start | bytes 589828
  34.5 14.5 %copy-start.18 = (s32[16]{0:T(128)S(1)}, s32[16]{0:T(128)}, u32[]{:S(2)}) copy-start(s32[16]{0:T(128)} %param.20) | copy-start | bytes 196
  34.5 15.5 %copy-start.21 = (s32[16]{0:T(128)S(1)}, s32[16]{0:T(128)}, u32[]{:S(2)}) copy-start(s32[16]{0:T(128)} %param.22) | copy-start | bytes 196
  34.5 424.6 %all-to-all-start = ((bf16[64,48,640]{2,1,0:T(8,128)(2,1)}), bf16[64,48,640]{2,1,0:T(8,128)(2,1)}, u32[]{:S(2)}, u32[]{:S(2)}) async-start(bf16[64,48,640]{2,1,0:T(8,128)(2,1)} %stack.11), calls=%async_computation | async-start | bytes 7864320 | tf_op jit(solution)/shard_map/all_to_all | solution.py:135
  48.7 4.0 copy-start.17
  48.7 410.4 %all-gather.2.cloned.1.call-start = ((), (), s32[]{:S(2)}) async-start(), calls=%async_computation.1 | async-start | bytes 1769472 | tf_op jit(solution)/shard_map/all_gather | solution.py:131
  57.2 3.7 copy-start.16
  57.2 3.7 copy-start.15
  58.2 4.1 copy-start.11
  66.5 220.4 %collective-permute-start.4 = (bf16[2,512,384]{1,2,0:T(8,128)(2,1)}, bf16[2,512,384]{1,2,0:T(8,128)(2,1)S(1)}, u32[]{:S(2)}, u32[]{:S(2)}) collective-permute-start(bf16[2,512,384]{1,2,0:T(8,128)(2,1)} %pad_maximum_fusion), channel_id=1, source_target_pairs={{0,24},{8,32},{16,40},{24,48},{32,56},{40,64},{48,72},{56,80},{64,... | collective-permute-start | bytes 2359304 | tf_op jit(solution)/shard_map/ppermute | solution.py:17
  185.9 141.6 %collective-permute-start.3 = (bf16[2,512,384]{1,2,0:T(8,128)(2,1)}, bf16[2,512,384]{1,2,0:T(8,128)(2,1)S(1)}, u32[]{:S(2)}, u32[]{:S(2)}) collective-permute-start(bf16[2,512,384]{1,2,0:T(8,128)(2,1)} %pad_maximum_fusion), channel_id=1, source_target_pairs={{16,0},{24,8},{32,16},{40,24},{48,32},{56,40},{64,48},{72,56},{80,... | collective-permute-start | bytes 2359304 | tf_op jit(solution)/shard_map/ppermute | solution.py:17
  188.4 141.7 %collective-permute-start.2 = (bf16[2,512,384]{1,2,0:T(8,128)(2,1)}, bf16[2,512,384]{1,2,0:T(8,128)(2,1)S(1)}, u32[]{:S(2)}, u32[]{:S(2)}) collective-permute-start(bf16[2,512,384]{1,2,0:T(8,128)(2,1)} %pad_maximum_fusion), channel_id=1, source_target_pairs={{0,16},{8,24},{16,32},{24,40},{32,48},{40,56},{48,64},{56,72},{64,... | collective-permute-start | bytes 2359304 | tf_op jit(solution)/shard_map/ppermute | solution.py:17
  210.9 120.2 %collective-permute-start.1 = (bf16[2,512,384]{1,2,0:T(8,128)(2,1)}, bf16[2,512,384]{1,2,0:T(8,128)(2,1)S(1)}, u32[]{:S(2)}, u32[]{:S(2)}) collective-permute-start(bf16[2,512,384]{1,2,0:T(8,128)(2,1)} %pad_maximum_fusion), channel_id=1, source_target_pairs={{8,0},{16,8},{24,16},{32,24},{40,32},{48,40},{56,48},{64,56},{72,6... | collective-permute-start | bytes 2359304 | tf_op jit(solution)/shard_map/ppermute | solution.py:17
  262.1 70.4 %collective-permute-start.10 = (bf16[2,512,384]{1,2,0:T(8,128)(2,1)}, bf16[2,512,384]{1,2,0:T(8,128)(2,1)S(1)}, u32[]{:S(2)}, u32[]{:S(2)}) collective-permute-start(bf16[2,512,384]{1,2,0:T(8,128)(2,1)} %pad_maximum_fusion), channel_id=1, source_target_pairs={{0,48},{8,56},{16,64},{24,72},{32,80},{40,88},{48,96},{56,104},{64... | collective-permute-start | bytes 2359304 | tf_op jit(solution)/shard_map/ppermute | solution.py:17
  286.9 66.2 %collective-permute-start = (bf16[2,512,384]{1,2,0:T(8,128)(2,1)}, bf16[2,512,384]{1,2,0:T(8,128)(2,1)S(1)}, u32[]{:S(2)}, u32[]{:S(2)}) collective-permute-start(bf16[2,512,384]{1,2,0:T(8,128)(2,1)} %pad_maximum_fusion), channel_id=1, source_target_pairs={{0,8},{8,16},{16,24},{24,32},{32,40},{40,48},{48,56},{56,64},{64,7... | collective-permute-start | bytes 2359304 | tf_op jit(solution)/shard_map/ppermute | solution.py:17
  327.6 26.6 %collective-permute-start.11 = (bf16[2,512,384]{1,2,0:T(8,128)(2,1)}, bf16[2,512,384]{1,2,0:T(8,128)(2,1)S(1)}, u32[]{:S(2)}, u32[]{:S(2)}) collective-permute-start(bf16[2,512,384]{1,2,0:T(8,128)(2,1)} %pad_maximum_fusion), channel_id=1, source_target_pairs={{48,0},{56,8},{64,16},{72,24},{80,32},{88,40},{96,48},{104,56},{11... | collective-permute-start | bytes 2359304 | tf_op jit(solution)/shard_map/ppermute | solution.py:17
  331.1 0.9 copy-start.1
  332.0 0.9 copy-start.3
  332.5 0.9 copy-start.4
  333.4 19.7 %copy-start.2 = (pred[256,512]{0,1:T(8,128)(4,1)S(1)}, pred[256,512]{0,1:T(8,128)(4,1)}, u32[]{:S(2)}) copy-start(pred[256,512]{0,1:T(8,128)(4,1)} %pad_add_fusion.11) | copy-start | bytes 393220
  333.9 19.7 %copy-start.5 = (pred[256,512]{0,1:T(8,128)(4,1)S(1)}, pred[256,512]{0,1:T(8,128)(4,1)}, u32[]{:S(2)}) copy-start(pred[256,512]{0,1:T(8,128)(4,1)} %pad_add_fusion.1) | copy-start | bytes 393220
  353.6 0.9 copy-start.7
  354.2 1.4 copy-start.6
  354.2 1.4 copy-start.12
  359.0 0.9 copy-start.10
  359.1 1.0 copy-start.13
  365.8 1.2 copy-start.19
  367.0 92.1 %copy-start.20 = (bf16[256,640]{1,0:T(8,128)(2,1)S(1)}, bf16[256,640]{1,0:T(8,128)(2,1)}, u32[]{:S(2)}) copy-start(bf16[256,640]{1,0:T(8,128)(2,1)} %param.17) | copy-start | bytes 983044
Sparse Core Ops, SparseCore 0:
  367.1 91.9 all-gather.1
